TPU v7x, 32 devices: a whole 2x2x4 slice. The times are simulated.
32 devices in a mesh: win: 2 (over x), wide: 8 (over z, y), narrow: 2 (over core).
Axes of the slice: x: 2, y: 2, z: 4, core: 2. Of those that a mesh axis runs over, the one named last changes fastest.
Arguments:
- window_data: float32 [384, 128, 256], P(('win', 'wide'), 'narrow'), parts along dimension 0, may hold values from -6 to 6
- factor_one: float32 [256, 48], P(('win', 'narrow')), parts along dimension 0, may hold values from -0.5 to 0.5
- factor_two: float32 [512, 48], P('win'), parts along dimension 0, may hold values from -0.375 to 0.375
- factor_three: float32 [384, 48], P(('win', 'wide')), parts along dimension 0, may hold values from -0.4375 to 0.4375
Outputs:
- basis_one: float32 [256, 48], P(('win', 'narrow')), parts along dimension 0
- basis_two: float32 [512, 48], P('win'), parts along dimension 0
- basis_three: float32 [384, 48], P(('win', 'wide')), parts along dimension 0
- core_unfolded: float32 [48, 4608], P(None, ('win', 'wide', 'narrow')), parts along dimension 1
There are 2 independent parts, one for each index of `win`. A program takes and returns all parts, laid end to end along the dimension named above; each array names one. Nothing has to cross between parts.
All inputs are finite; a program needn't handle non-finite values.
Results may differ from a plain program's by a relative error of at most 0.0003.
Values sent between devices are 32-bit elements; how exact they have to be, the bound alone decides.
No kernel may reach another device: no remote copies, remote signals or barrier semaphores. Data moves between devices by JAX's collectives and lax.ppermute only.
A program may use at most 64 MiB of HBM per device.

v0:
```python
import jax
import jax.numpy as jnp
from jax import lax
from jax.sharding import PartitionSpec as P

highest = lax.Precision.HIGHEST


def contract(form, left, right):
    return jnp.einsum(form, left, right, precision=highest)


def orthonormal(basis, gram):
    lower = jnp.linalg.cholesky(gram)
    return lax.linalg.triangular_solve(lower, basis, left_side=False, lower=True, transpose_a=True)


def full_core(partial_value):
    flat = partial_value.reshape(
        partial_value.shape[0], partial_value.shape[1] * partial_value.shape[2]
    )
    shares = lax.psum_scatter(flat, ("wide", "narrow"), scatter_dimension=1, tiled=True)
    whole = lax.all_gather(shares, ("wide", "narrow"), axis=1, tiled=True)
    return whole.reshape(partial_value.shape)


def on_device(window_data, factor_one, factor_two, factor_three):
    rank = factor_one.shape[1]
    along_two = contract("kij,jb->kib", window_data, factor_two)
    unfold_part = contract("kib,kc->ibc", along_two, factor_three).reshape(
        along_two.shape[1], rank * rank
    )
    unfold_rows = lax.psum_scatter(unfold_part, "wide", scatter_dimension=1, tiled=True)
    weights_one = lax.psum(jnp.dot(unfold_rows.T, factor_one, precision=highest), "narrow")
    product_one = lax.psum(jnp.dot(unfold_rows, weights_one, precision=highest), "wide")
    gram_one = lax.psum(jnp.dot(product_one.T, product_one, precision=highest), "narrow")
    basis_one = orthonormal(product_one, gram_one)
    along_one = contract("kij,ia->kaj", window_data, basis_one)
    core_two = full_core(
        contract("kab,kc->abc", contract("kaj,jb->kab", along_one, factor_two), factor_three)
    )
    spread_two = contract("abc,kc->kab", core_two, factor_three)
    product_two = lax.psum(contract("kaj,kab->jb", along_one, spread_two), ("wide", "narrow"))
    basis_two = orthonormal(product_two, jnp.dot(product_two.T, product_two, precision=highest))
    along_new = contract("kij,jb->kib", window_data, basis_two)
    unfold_three = contract("kib,ia->kab", along_new, basis_one)
    core_three = full_core(contract("kab,kc->abc", unfold_three, factor_three))
    product_three = lax.psum(contract("kab,abc->kc", unfold_three, core_three), "narrow")
    gram_three = lax.psum(jnp.dot(product_three.T, product_three, precision=highest), "wide")
    basis_three = orthonormal(product_three, gram_three)
    core_part = contract("kab,kc->abc", unfold_three, basis_three).reshape(rank, rank * rank)
    core_shares = lax.psum_scatter(core_part, ("wide", "narrow"), scatter_dimension=1, tiled=True)
    return (basis_one, basis_two, basis_three, core_shares)


def solution(mesh):
    return jax.shard_map(
        on_device,
        mesh=mesh,
        in_specs=(
            P(("win", "wide"), "narrow", None),
            P(("win", "narrow"), None),
            P("win", None),
            P(("win", "wide"), None),
        ),
        out_specs=(
            P(("win", "narrow"), None),
            P("win", None),
            P(("win", "wide"), None),
            P(None, ("win", "wide", "narrow")),
        ),
        check_vma=False,
    )
```

profile of v0, /device:TPU:0, one launch (start us, length us, event | category | flops | bytes accessed | tf_op | source)
XLA Modules:
  0.0 505.6 jit_solution(5925950153966513324)
XLA Ops:
  8.6 3.1 fusion.12
  13.9 67.9 %reduce-scatter.11.cloned.1.call-done = f32[64,288]{0,1:T(8,128)} async-done(((f32[64,2304]{0,1:T(8,128)}), f32[64,288]{0,1:T(8,128)}) %reduce-scatter.11.cloned.1.call-update) | async-done | bytes 73744 | tf_op jit(solution)/shard_map/reduce_scatter | solution.py:33
  83.1 3.5 psum.42
  87.7 34.9 %psum.43 = f32[64,48]{0,1:T(8,128)S(1)} all-reduce(f32[64,48]{0,1:T(8,128)S(1)} %fusion.35), channel_id=1, replica_groups=mesh['win'=2,'wide'=8,'narrow'=2] {'wide'}, use_global_device_ids=true, to_apply=%region_2.0 | all-reduce | flops 3072 | bytes 24576 | tf_op jit(solution)/shard_map/psum | solution.py:35
  122.8 3.4 psum.44
  126.3 4.4 cholesky.59
  132.0 3.7 custom-call.11
  138.7 3.1 fusion.31
  141.8 2.7 copy.45
  144.6 55.5 %reduce-scatter.13.cloned.1.call-done = f32[144,48]{1,0:T(8,128)} async-done(((f32[2304,48]{1,0:T(8,128)}), f32[144,48]{1,0:T(8,128)}) %reduce-scatter.13.cloned.1.call-update) | async-done | bytes 27664
  201.0 21.8 %all-gather = f32[16,144,48]{1,2,0:T(8,128)S(1)} all-gather(f32[1,144,48]{1,2,0:T(8,128)S(1)} %bitcast.116), channel_id=1, replica_groups=mesh['win'=2,'wide'=8,'narrow'=2] {'wide','narrow'}, dimensions={0}, use_global_device_ids=true | all-gather | bytes 470016 | tf_op jit(solution)/shard_map/all_gather | solution.py:23
  224.4 2.7 reshape.42
  227.2 4.7 convolution_bitcast_fusion.3
  233.1 57.9 %psum.45 = f32[256,48]{0,1:T(8,128)S(1)} all-reduce(f32[256,48]{0,1:T(8,128)S(1)} %convolution_bitcast_fusion.4), channel_id=1, replica_groups=mesh['win'=2,'wide'=8,'narrow'=2] {'wide','narrow'}, use_global_device_ids=true, to_apply=%region_7.0 | all-reduce | flops 12288 | bytes 98304 | tf_op jit(solution)/shard_map/psum | solution.py:43
  291.3 4.4 cholesky.70
  297.0 3.7 custom-call.12
  301.0 2.3 convolution_bitcast_fusion.2
  309.1 55.5 %reduce-scatter.15.cloned.1.call-done = f32[144,48]{1,0:T(8,128)} async-done(((f32[2304,48]{1,0:T(8,128)}), f32[144,48]{1,0:T(8,128)}) %reduce-scatter.15.cloned.1.call-update) | async-done | bytes 27664
  365.5 21.8 %all-gather.1 = f32[16,144,48]{1,2,0:T(8,128)S(1)} all-gather(f32[1,144,48]{1,2,0:T(8,128)S(1)} %bitcast.117), channel_id=1, replica_groups=mesh['win'=2,'wide'=8,'narrow'=2] {'wide','narrow'}, dimensions={0}, use_global_device_ids=true | all-gather | bytes 470016 | tf_op jit(solution)/shard_map/all_gather | solution.py:23
  391.9 3.5 psum.46
  395.6 33.0 %psum.47 = f32[48,48]{0,1:T(8,128)S(1)} all-reduce(f32[48,48]{0,1:T(8,128)S(1)} %fusion.38), channel_id=1, replica_groups=mesh['win'=2,'wide'=8,'narrow'=2] {'wide'}, use_global_device_ids=true, to_apply=%region_10.12 | all-reduce | flops 2304 | bytes 18432 | tf_op jit(solution)/shard_map/psum | solution.py:49
  428.7 4.4 cholesky.81
  434.4 3.7 custom-call.13
  441.9 55.6 %reduce-scatter.17.cloned.1.call-done = f32[144,48]{1,0:T(8,128)} async-done(((f32[2304,48]{1,0:T(8,128)}), f32[144,48]{1,0:T(8,128)}) %reduce-scatter.17.cloned.1.call-update) | async-done | bytes 27664
  (65 shorter events, 34.3 us)
Async XLA Ops:
  7.2 1.4 copy-start
  7.2 4.5 copy-start.3
  7.2 74.7 %reduce-scatter.11.cloned.1.call-start = ((), (), s32[]{:S(2)}) async-start(), calls=%async_computation.4 | async-start | bytes 1327104 | tf_op jit(solution)/shard_map/reduce_scatter | solution.py:33
  11.7 70.2 %copy-start.7 = (f32[64,48]{0,1:T(8,128)S(1)}, f32[64,48]{0,1:T(8,128)}, u32[]{:S(2)}) copy-start(f32[64,48]{0,1:T(8,128)} %param.6) | copy-start | bytes 36868
  13.9 186.2 %reduce-scatter.13.cloned.1.call-start = ((), (), s32[]{:S(2)}) async-start(), calls=%async_computation.5 | async-start | bytes 1253376
  135.9 1.1 copy-start.1
  136.0 1.1 copy-start.5
  144.5 220.0 %reduce-scatter.15.cloned.1.call-start = ((), (), s32[]{:S(2)}) async-start(), calls=%async_computation.6 | async-start | bytes 1253376
  297.0 6.3 %copy-start.2 = (f32[64,48]{0,1:T(8,128)S(1)}, f32[64,48]{0,1:T(8,128)}, u32[]{:S(2)}) copy-start(f32[64,48]{0,1:T(8,128)} %copy-done.1) | copy-start | bytes 36868
  301.0 4.5 copy-start.4
  309.0 188.4 %reduce-scatter.17.cloned.1.call-start = ((), (), s32[]{:S(2)}) async-start(), calls=%async_computation.7 | async-start | bytes 1253376
  438.3 3.6 copy-start.6
Sparse Core Ops, SparseCore 0:
  14.0 67.8 reduce-scatter.10
  144.7 55.3 reduce-scatter.12
  309.1 55.3 reduce-scatter.14
  442.0 55.4 reduce-scatter.16
where the time goes:
time: 506 us
  waiting for transfers between devices  235 us (46%)
  blocking collectives  180 us (36%)
  matrix products  30.3 us (6%)
  other arithmetic  28.2 us (6%)
  local copies, waits for them, and re-layouts  18.5 us (4%)
  between operations  14.1 us (3%)
    unnamed x7, waiting for transfers between devices  167 us
    reduce_scatter x1, waiting for transfers between devices, on_device(): lax.psum_scatter(unfold_part, 'wide', scatter_dimension=1, tiled=True)  67.9 us
    psum x1, blocking collectives, on_device(): lax.psum(contract('kaj,kab->jb', along_one, spread_two), ('wide', 'narrow'))  57.9 us
    all_gather x2, blocking collectives, full_core(): whole = lax.all_gather(shares, ('wide', 'narrow'), axis=1, tiled=True)  43.6 us
    psum x1, blocking collectives, on_device(): lax.psum(jnp.dot(unfold_rows, weights_one, precision=highest), 'wide')  34.9 us
    psum x1, blocking collectives, on_device(): lax.psum(jnp.dot(product_three.T, product_three, precision=highest), 'wide')  33 us
    dot_general x12, matrix products, contract(): return jnp.einsum(form, left, right, precision=highest)  26.7 us
    another operation x9, other arithmetic, orthonormal(): lower = jnp.linalg.cholesky(gram)  15.2 us
  transfers between devices with their start and end apart: 4, of which 4 were waited for; matrix products, arithmetic and copies ran while one was open for 0% of the time, Pallas kernels for 0%

commit v1 on v0

--- a/solution.py
+++ b/solution.py
@@ -40,7 +40,9 @@
         contract("kab,kc->abc", contract("kaj,jb->kab", along_one, factor_two), factor_three)
     )
     spread_two = contract("abc,kc->kab", core_two, factor_three)
-    product_two = lax.psum(contract("kaj,kab->jb", along_one, spread_two), ("wide", "narrow"))
+    product_two = jnp.sum(
+        lax.all_gather(contract("kaj,kab->jb", along_one, spread_two), ("wide", "narrow")), axis=0
+    )
     basis_two = orthonormal(product_two, jnp.dot(product_two.T, product_two, precision=highest))
     along_new = contract("kij,jb->kib", window_data, basis_two)
     unfold_three = contract("kib,ia->kab", along_new, basis_one)

time: 506 us -> 470 us (0.929)
  blocking collectives: 180 us -> 141 us
    psum x1 -> x0, blocking collectives: 57.9 us -> none  [on_device(): lax.psum(contract('kaj,kab->jb', along_one, spread_two), ('wide', 'narrow'))]
    all_gather x0 -> x1, blocking collectives: none -> 19.6 us  [on_device(): lax.all_gather(contract('kaj,kab->jb', along_one, spread_two), ('wide', '...]
    unnamed x24 -> x25, local copies, waits for them, and re-layouts: 12.9 us -> 13.1 us
where the time goes in v1:
time: 470 us; the launch traced here: 469 us
  waiting for transfers between devices  236 us (50%)
  blocking collectives  141 us (30%)
  matrix products  30.3 us (6%)
  other arithmetic  28.3 us (6%)
  local copies, waits for them, and re-layouts  18.8 us (4%)
  between operations  14.1 us (3%)
    unnamed x7, waiting for transfers between devices  168 us
    reduce_scatter x1, waiting for transfers between devices, on_device(): lax.psum_scatter(unfold_part, 'wide', scatter_dimension=1, tiled=True)  67.9 us
    all_gather x2, blocking collectives, full_core(): whole = lax.all_gather(shares, ('wide', 'narrow'), axis=1, tiled=True)  43.4 us
    psum x1, blocking collectives, on_device(): lax.psum(jnp.dot(unfold_rows, weights_one, precision=highest), 'wide')  34.9 us
    psum x1, blocking collectives, on_device(): lax.psum(jnp.dot(product_three.T, product_three, precision=highest), 'wide')  33.3 us
    dot_general x12, matrix products, contract(): return jnp.einsum(form, left, right, precision=highest)  26.7 us
    all_gather x1, blocking collectives, on_device(): lax.all_gather(contract('kaj,kab->jb', along_one, spread_two), ('wide', '...  19.6 us
    another operation x9, other arithmetic, orthonormal(): lower = jnp.linalg.cholesky(gram)  15.2 us
  transfers between devices with their start and end apart: 4, of which 4 were waited for; matrix products, arithmetic and copies ran while one was open for 0% of the time, Pallas kernels for 0%

profile of v1, /device:TPU:0, one launch (start us, length us, event | category | flops | bytes accessed | tf_op | source)
XLA Modules:
  0.0 469.4 jit_solution(1440078477972940593)
XLA Ops:
  8.6 3.1 fusion.12
  13.9 67.9 %reduce-scatter.11.cloned.1.call-done = f32[64,288]{0,1:T(8,128)} async-done(((f32[64,2304]{0,1:T(8,128)}), f32[64,288]{0,1:T(8,128)}) %reduce-scatter.11.cloned.1.call-update) | async-done | bytes 73744 | tf_op jit(solution)/shard_map/reduce_scatter | solution.py:33
  83.1 3.5 psum.35
  87.7 34.9 %psum.36 = f32[64,48]{0,1:T(8,128)S(1)} all-reduce(f32[64,48]{0,1:T(8,128)S(1)} %fusion.35), channel_id=1, replica_groups=mesh['win'=2,'wide'=8,'narrow'=2] {'wide'}, use_global_device_ids=true, to_apply=%region_2.0 | all-reduce | flops 3072 | bytes 24576 | tf_op jit(solution)/shard_map/psum | solution.py:35
  122.8 3.4 psum.37
  126.3 4.4 cholesky.59
  132.0 3.7 custom-call.11
  138.7 3.1 fusion.31
  141.8 2.7 copy.45
  144.6 55.5 %reduce-scatter.13.cloned.1.call-done = f32[144,48]{1,0:T(8,128)} async-done(((f32[2304,48]{1,0:T(8,128)}), f32[144,48]{1,0:T(8,128)}) %reduce-scatter.13.cloned.1.call-update) | async-done | bytes 27664
  201.0 21.8 %all-gather.1 = f32[16,144,48]{1,2,0:T(8,128)S(1)} all-gather(f32[1,144,48]{1,2,0:T(8,128)S(1)} %bitcast.122), channel_id=1, replica_groups=mesh['win'=2,'wide'=8,'narrow'=2] {'wide','narrow'}, dimensions={0}, use_global_device_ids=true | all-gather | bytes 470016 | tf_op jit(solution)/shard_map/all_gather | solution.py:23
  224.4 2.7 reshape.42
  227.2 4.7 %convolution_bitcast_fusion.3 = f32[24,48,48]{2,0,1:T(8,128)S(1)} fusion(f32[48,48,48]{2,1,0:T(8,128)} %reshape.42, f32[24,48]{1,0:T(8,128)S(1)} %copy-done.3), kind=kOutput, calls=%fused_computation.3 | convolution fusion | flops 31850496 | bytes 668160 | tf_op jit(solution)/shard_map/abc,kc->kab/dot_general | solution.py:10
  233.1 19.6 %all-gather = f32[4096,48]{0,1:T(8,128)S(1)} all-gather(f32[256,48]{0,1:T(8,128)S(1)} %convolution_bitcast_fusion.4), channel_id=2, replica_groups=mesh['win'=2,'wide'=8,'narrow'=2] {'wide','narrow'}, dimensions={0}, use_global_device_ids=true | all-gather | bytes 835584 | tf_op jit(solution)/shard_map/all_gather | solution.py:44
  253.4 4.4 cholesky.70
  259.1 3.7 custom-call.12
  263.0 2.3 convolution_bitcast_fusion.2
  271.1 57.4 %reduce-scatter.15.cloned.1.call-done = f32[144,48]{1,0:T(8,128)} async-done(((f32[2304,48]{1,0:T(8,128)}), f32[144,48]{1,0:T(8,128)}) %reduce-scatter.15.cloned.1.call-update) | async-done | bytes 27664
  329.5 21.6 %all-gather.2 = f32[16,144,48]{1,2,0:T(8,128)S(1)} all-gather(f32[1,144,48]{1,2,0:T(8,128)S(1)} %bitcast.123), channel_id=1, replica_groups=mesh['win'=2,'wide'=8,'narrow'=2] {'wide','narrow'}, dimensions={0}, use_global_device_ids=true | all-gather | bytes 470016 | tf_op jit(solution)/shard_map/all_gather | solution.py:23
  355.6 3.5 psum.38
  359.3 33.3 %psum.39 = f32[48,48]{0,1:T(8,128)S(1)} all-reduce(f32[48,48]{0,1:T(8,128)S(1)} %fusion.38), channel_id=1, replica_groups=mesh['win'=2,'wide'=8,'narrow'=2] {'wide'}, use_global_device_ids=true, to_apply=%region_10.12 | all-reduce | flops 2304 | bytes 18432 | tf_op jit(solution)/shard_map/psum | solution.py:51
  392.7 4.4 cholesky.81
  398.4 3.7 custom-call.13
  405.8 55.5 %reduce-scatter.17.cloned.1.call-done = f32[144,48]{1,0:T(8,128)} async-done(((f32[2304,48]{1,0:T(8,128)}), f32[144,48]{1,0:T(8,128)}) %reduce-scatter.17.cloned.1.call-update) | async-done | bytes 27664
  (67 shorter events, 34.7 us)
Async XLA Ops:
  7.2 1.4 copy-start
  7.2 4.5 copy-start.3
  7.2 74.7 %reduce-scatter.11.cloned.1.call-start = ((), (), s32[]{:S(2)}) async-start(), calls=%async_computation.4 | async-start | bytes 1327104 | tf_op jit(solution)/shard_map/reduce_scatter | solution.py:33
  11.7 70.2 %copy-start.7 = (f32[64,48]{0,1:T(8,128)S(1)}, f32[64,48]{0,1:T(8,128)}, u32[]{:S(2)}) copy-start(f32[64,48]{0,1:T(8,128)} %param.6) | copy-start | bytes 36868
  13.9 186.2 %reduce-scatter.13.cloned.1.call-start = ((), (), s32[]{:S(2)}) async-start(), calls=%async_computation.5 | async-start | bytes 1253376
  135.9 1.1 copy-start.1
  136.0 1.1 copy-start.5
  144.5 184.0 %reduce-scatter.15.cloned.1.call-start = ((), (), s32[]{:S(2)}) async-start(), calls=%async_computation.6 | async-start | bytes 1253376
  259.1 6.3 %copy-start.2 = (f32[64,48]{0,1:T(8,128)S(1)}, f32[64,48]{0,1:T(8,128)}, u32[]{:S(2)}) copy-start(f32[64,48]{0,1:T(8,128)} %copy-done.1) | copy-start | bytes 36868
  263.0 4.5 copy-start.4
  271.1 190.2 %reduce-scatter.17.cloned.1.call-start = ((), (), s32[]{:S(2)}) async-start(), calls=%async_computation.7 | async-start | bytes 1253376
  402.2 3.6 copy-start.6
Sparse Core Ops, SparseCore 0:
  14.0 67.8 reduce-scatter.10
  144.7 55.3 reduce-scatter.12
  271.2 57.2 reduce-scatter.14
  405.9 55.3 reduce-scatter.16
